TPU v7x, 256 devices: a whole 4x4x8 slice. The times are simulated.
256 devices in a mesh: req: 64 (over x_lo, y, z), ctx: 4 (over x_hi, core).
Axes of the slice: x: 4 (x_hi: 2, x_lo: 2; x = x_hi * 2 + x_lo), y: 4, z: 8, core: 2. Of those that a mesh axis runs over, the one named last changes fastest.
Arguments:
- q_nope: bfloat16 [64, 128, 8192], P('req'), may hold values from -6 to 6
- q_rope: bfloat16 [64, 128, 4096], P('req'), may hold values from -600 to 600
- cache_latent: bfloat16 [64, 1024, 512], P('req', 'ctx'), may hold values from -6 to 6
- cache_rope: bfloat16 [64, 1024, 64], P('req', 'ctx'), may hold values from -4 to 4
- new_latent: bfloat16 [64, 128, 512], P('req', 'ctx'), may hold values from -6 to 6
- new_rope: bfloat16 [64, 128, 64], P('req', 'ctx'), may hold values from -8 to 8
- lengths: int32 [64, 4], P('req', 'ctx'), may hold values from 64 to 256, as said below
- w_key: bfloat16 [512, 8192], P(None, 'ctx'), may hold values from -0.25 to 0.25
- w_value: bfloat16 [512, 8192], P(None, 'ctx'), may hold values from -0.25 to 0.25
Outputs:
- attended: bfloat16 [64, 128, 8192], P('req', None, 'ctx')
Inputs may be any that keep to these rules, and one draw needn't show every extreme that they name: lengths[r, g] counts the live cached rows at the start of request r's slots in context group g; all cached rows precede the new tokens; some entry equals 256 in every draw.
All inputs are finite; a program needn't handle non-finite values.
Results may differ from a plain program's by a relative error of at most 0.015.
Values may be sent and summed in bfloat16 or wider, within the bound.
A program may use at most 128 MiB of HBM per device.

v0:
```python
import math
import jax
import jax.numpy as jnp
from jax import lax
from jax.sharding import PartitionSpec as P

DR = 64
DH = 128
DV = 128
HEADS = 64
GROUP = 4
BLOCK = 256
blocked_score = -1e30


def expand_block(
    lat_rows, rope_keys, visible, query_nope, query_rope, weight_key, weight_value, running
):
    running_max, running_sum, running_out = running
    row_count = lat_rows.shape[0]
    score_scale = 1.0 / math.sqrt(DH + DR)
    key_rows = jnp.dot(lat_rows, weight_key, preferred_element_type=jnp.float32).astype(
        jnp.bfloat16
    )
    value_rows = jnp.dot(lat_rows, weight_value, preferred_element_type=jnp.float32).astype(
        jnp.bfloat16
    )
    key_rows = key_rows.reshape(row_count, GROUP, DH)
    value_rows = value_rows.reshape(row_count, GROUP, DV)
    scores = jnp.einsum("qhd,khd->qhk", query_nope, key_rows, preferred_element_type=jnp.float32)
    scores = scores + jnp.einsum(
        "qhd,kd->qhk", query_rope, rope_keys, preferred_element_type=jnp.float32
    )
    scores = jnp.where(visible[:, None, :], scores * score_scale, blocked_score)
    new_max = jnp.maximum(running_max, jnp.max(scores, axis=-1))
    factor = jnp.exp(running_max - new_max)
    weights = jnp.where(visible[:, None, :], jnp.exp(scores - new_max[..., None]), 0.0)
    running_sum = running_sum * factor + jnp.sum(weights, axis=-1)
    running_out = running_out * factor[..., None] + jnp.einsum(
        "qhk,khd->qhd", weights.astype(jnp.bfloat16), value_rows, preferred_element_type=jnp.float32
    )
    return (new_max, running_sum, running_out)


def start_running(query_count):
    return (
        jnp.full((query_count, GROUP), blocked_score, jnp.float32),
        jnp.zeros((query_count, GROUP), jnp.float32),
        jnp.zeros((query_count, GROUP, DV), jnp.float32),
    )


def cached_pass(
    running, query_nope, query_rope, weight_key, weight_value, cache_rows, cache_keys, live_rows
):

    def advance(block_index, running):
        offset = block_index * BLOCK
        visible = (offset + jnp.arange(BLOCK, dtype=jnp.int32))[None, :] < live_rows
        visible = jnp.broadcast_to(visible, (query_nope.shape[0], BLOCK))
        return expand_block(
            cache_rows,
            cache_keys,
            visible,
            query_nope,
            query_rope,
            weight_key,
            weight_value,
            running,
        )

    block_count = (live_rows + BLOCK - 1) // BLOCK
    return lax.fori_loop(0, block_count, advance, running)


def fresh_pass(
    running, query_nope, query_rope, weight_key, weight_value, fresh_rows, fresh_keys, fresh_first
):
    query_count = query_nope.shape[0]
    fresh_index = fresh_first + jnp.arange(fresh_rows.shape[0], dtype=jnp.int32)
    visible = fresh_index[None, :] <= jnp.arange(query_count, dtype=jnp.int32)[:, None]
    return expand_block(
        fresh_rows, fresh_keys, visible, query_nope, query_rope, weight_key, weight_value, running
    )


def shards(q_nope, q_rope, cache_latent, cache_rope, new_latent, new_rope, lengths, w_key, w_value):
    ctx_count = lax.axis_size("ctx")
    ctx_index = lax.axis_index("ctx")
    queries = q_nope[0]
    rotary = q_rope[0]
    query_count = queries.shape[0]
    width_key = GROUP * DH
    width_value = GROUP * DV
    heads_here = HEADS // ctx_count
    groups = HEADS // GROUP
    fresh_rows = new_latent[0]
    fresh_first = ctx_index * fresh_rows.shape[0]
    live_rows = lengths[0, 0]
    full_key, full_value = (
        lax.all_gather(w_key, "ctx", axis=1, tiled=True),
        lax.all_gather(w_value, "ctx", axis=1, tiled=True),
    )
    maxima = []
    sums = []
    outputs = []
    for group_index in range(groups):
        weight_key = full_key[:, group_index * width_key : (group_index + 1) * width_key]
        weight_value = full_value[:, group_index * width_value : (group_index + 1) * width_value]
        query_nope = queries[:, group_index * GROUP * DH : (group_index + 1) * GROUP * DH].reshape(
            query_count, GROUP, DH
        )
        query_rope = rotary[:, group_index * GROUP * DR : (group_index + 1) * GROUP * DR].reshape(
            query_count, GROUP, DR
        )
        running = start_running(query_count)
        running = cached_pass(
            running,
            query_nope,
            query_rope,
            weight_key,
            weight_value,
            cache_latent[0],
            cache_rope[0],
            live_rows,
        )
        group_max, group_sum, group_out = fresh_pass(
            running,
            query_nope,
            query_rope,
            weight_key,
            weight_value,
            fresh_rows,
            new_rope[0],
            fresh_first,
        )
        maxima.append(group_max)
        sums.append(group_sum)
        outputs.append(group_out)
    running_max = jnp.concatenate(maxima, axis=1)
    running_sum = jnp.concatenate(sums, axis=1)
    running_out = jnp.concatenate(outputs, axis=1)
    overall_max = lax.pmax(running_max.astype(jnp.bfloat16), "ctx").astype(running_max.dtype)
    factor = jnp.exp(running_max - overall_max)
    numerator, denominator = (
        lax.psum_scatter(
            (running_out * factor[..., None]).reshape(query_count, HEADS * DV).astype(jnp.bfloat16),
            "ctx",
            scatter_dimension=1,
            tiled=True,
        ).astype(jnp.float32),
        lax.psum_scatter(
            (running_sum * factor).astype(jnp.bfloat16), "ctx", scatter_dimension=1, tiled=True
        ).astype(jnp.float32),
    )
    numerator = numerator.reshape(query_count, heads_here, DV)
    attended = (numerator / denominator[..., None]).reshape(query_count, heads_here * DV)
    return attended.astype(jnp.bfloat16)[None]


def solution(mesh):
    return jax.shard_map(
        shards,
        mesh=mesh,
        in_specs=(
            P("req", None, None),
            P("req", None, None),
            P("req", "ctx", None),
            P("req", "ctx", None),
            P("req", "ctx", None),
            P("req", "ctx", None),
            P("req", "ctx"),
            P(None, "ctx"),
            P(None, "ctx"),
        ),
        out_specs=P("req", None, "ctx"),
        check_vma=False,
    )
```

profile of v0, /device:TPU:1, one launch (start us, length us, event | category | flops | bytes accessed | tf_op | source)
XLA Modules:
  0.0 420.9 jit_solution(1115684594973445940)
XLA Ops:
  18.6 3.2 copy.204
  34.6 43.7 %all-gather.3.cloned.1.call-done = bf16[512,8192]{1,0:T(8,128)(2,1)} async-done(((bf16[512,2048]{1,0:T(8,128)(2,1)}), bf16[512,8192]{1,0:T(8,128)(2,1)}) %all-gather.3.cloned.1.call-update) | async-done | bytes 8388624 | tf_op jit(solution)/shard_map/all_gather | solution.py:101
  82.5 61.9 %all-gather.5.cloned.1.call-done = bf16[512,8192]{1,0:T(8,128)(2,1)} async-done(((bf16[512,2048]{1,0:T(8,128)(2,1)}), bf16[512,8192]{1,0:T(8,128)(2,1)}) %all-gather.5.cloned.1.call-update) | async-done | bytes 8388624 | tf_op jit(solution)/shard_map/all_gather | solution.py:102
  146.4 3.9 while.271
  157.9 5.1 %while.269 = (s32[]{:T(128)}, f32[128,4]{0,1:T(4,128)}, f32[128,4]{0,1:T(4,128)}, f32[128,4,128]{2,0,1:T(8,128)S(1)}, s32[]{:T(128)}, /*index=5*/s32[]{:T(128)},...) while((s32[]{:T(128)}, f32[128,4]{0,1:T(4,128)}, ...), condition=%wide.region_68.69_spmd, body=%wide.region_65.68_spmd.sunk | while | flops 85329408 | bytes 3933329 | solution.py:73
  163.9 2.2 fusion.676
  176.0 2.2 fusion.685
  183.8 1.8 while.268
  186.5 2.2 fusion.690
  193.5 1.9 while.267
  202.4 2.0 while.266
  204.6 2.2 fusion.688
  211.6 1.9 while.265
  220.5 1.8 while.264
  222.5 2.2 fusion.686
  229.5 1.9 while.263
  238.4 1.8 while.262
  240.4 2.2 fusion.683
  271.3 2.0 while.258
  288.5 1.8 while.256
  303.2 12.5 %pmax.7 = bf16[128,64]{0,1:T(8,128)(2,1)S(1)} all-reduce(bf16[128,64]{0,1:T(8,128)(2,1)S(1)} %convert_element_type.488), channel_id=1, replica_groups=mesh['req'=64,'ctx'=4] {'ctx'}, use_global_device_ids=true, to_apply=%region_80.81 | all-reduce | flops 8192 | bytes 32768 | tf_op jit(solution)/shard_map/pmax | solution.py:143
  363.8 3.0 copy.301
  367.6 44.2 %reduce-scatter.3.cloned.1.call-done = bf16[128,2048]{1,0:T(8,128)(2,1)} async-done(((bf16[128,8192]{1,0:T(8,128)(2,1)}), bf16[128,2048]{1,0:T(8,128)(2,1)}) %reduce-scatter.3.cloned.1.call-update) | async-done | bytes 524304 | tf_op jit(solution)/shard_map/reduce_scatter | solution.py:146
  412.2 2.2 fusion.337
  (583 shorter events, 228.7 us)
Async XLA Ops:
  6.5 74.6 %copy-start = (bf16[1,256,512]{2,1,0:T(8,128)(2,1)S(1)}, bf16[1,256,512]{2,1,0:T(8,128)(2,1)}, u32[]{:S(2)}) copy-start(bf16[1,256,512]{2,1,0:T(8,128)(2,1)} %param.43) | copy-start | bytes 786436
  6.5 71.7 %all-gather.3.cloned.1.call-start = ((), (), s32[]{:S(2)}) async-start(), calls=%async_computation.2 | async-start | bytes 10485760 | tf_op jit(solution)/shard_map/all_gather | solution.py:101
  7.3 137.1 %all-gather.5.cloned.1.call-start = ((), (), s32[]{:S(2)}) async-start(), calls=%async_computation.3 | async-start | bytes 10485760 | tf_op jit(solution)/shard_map/all_gather | solution.py:102
  8.0 358.8 %reduce-scatter.5.cloned.1.call-start = ((), (), s32[]{:S(2)}) async-start(), calls=%async_computation.5 | async-start | bytes 20480 | tf_op jit(solution)/shard_map/reduce_scatter | solution.py:152
  8.7 69.5 %copy-start.2 = (bf16[1,32,512]{2,1,0:T(8,128)(2,1)S(1)}, bf16[1,32,512]{2,1,0:T(8,128)(2,1)}, u32[]{:S(2)}) copy-start(bf16[1,32,512]{2,1,0:T(8,128)(2,1)} %param.45) | copy-start | bytes 98308
  17.3 129.1 %copy-start.1 = (bf16[1,256,64]{1,2,0:T(8,128)(2,1)S(1)}, bf16[1,256,64]{1,2,0:T(8,128)(2,1)}, u32[]{:S(2)}) copy-start(bf16[1,256,64]{1,2,0:T(8,128)(2,1)} %param.44) | copy-start | bytes 98308
  22.9 122.8 %copy-start.14 = (bf16[128,512]{0,1:T(8,128)(2,1)}, bf16[128,512]{0,1:T(8,128)(2,1)S(1)}, u32[]{:S(2)}) copy-start(bf16[128,512]{0,1:T(8,128)(2,1)S(1)} %get-tuple-element.3014) | copy-start | bytes 393220
  288.5 32.1 %copy-start.40 = (f32[128,4,32]{0,2,1:T(8,128)S(1)}, f32[128,4,32]{0,2,1:T(8,128)}, u32[]{:S(2)}) copy-start(f32[128,4,32]{0,2,1:T(8,128)} %get-tuple-element.3032) | copy-start | bytes 196612
  290.4 51.8 %copy-start.39 = (f32[128,4,128]{0,2,1:T(8,128)S(1)}, f32[128,4,128]{0,2,1:T(8,128)}, u32[]{:S(2)}) copy-start(f32[128,4,128]{0,2,1:T(8,128)} %copy.239) | copy-start | bytes 786436
  290.4 56.4 %copy-start.38 = (f32[128,4,128]{0,2,1:T(8,128)S(1)}, f32[128,4,128]{0,2,1:T(8,128)}, u32[]{:S(2)}) copy-start(f32[128,4,128]{0,2,1:T(8,128)} %copy.251) | copy-start | bytes 786436
  290.4 61.1 %copy-start.37 = (f32[128,4,128]{0,2,1:T(8,128)S(1)}, f32[128,4,128]{0,2,1:T(8,128)}, u32[]{:S(2)}) copy-start(f32[128,4,128]{0,2,1:T(8,128)} %copy.263) | copy-start | bytes 786436
  290.4 65.8 %copy-start.36 = (f32[128,4,128]{0,2,1:T(8,128)S(1)}, f32[128,4,128]{0,2,1:T(8,128)}, u32[]{:S(2)}) copy-start(f32[128,4,128]{0,2,1:T(8,128)} %copy.275) | copy-start | bytes 786436
  293.4 34.9 %copy-start.76 = (f32[128,4]{0,1:T(4,128)}, f32[128,4]{0,1:T(4,128)S(1)}, u32[]{:S(2)}) copy-start(f32[128,4]{0,1:T(4,128)S(1)} %max.143) | copy-start | bytes 6148
  294.8 33.6 %copy-start.78 = (f32[128,4]{0,1:T(4,128)}, f32[128,4]{0,1:T(4,128)S(1)}, u32[]{:S(2)}) copy-start(f32[128,4]{0,1:T(4,128)S(1)} %max.142) | copy-start | bytes 6148
  295.5 32.9 %copy-start.80 = (f32[128,4]{0,1:T(4,128)}, f32[128,4]{0,1:T(4,128)S(1)}, u32[]{:S(2)}) copy-start(f32[128,4]{0,1:T(4,128)S(1)} %max.141) | copy-start | bytes 6148
  296.1 32.2 %copy-start.82 = (f32[128,4]{0,1:T(4,128)}, f32[128,4]{0,1:T(4,128)S(1)}, u32[]{:S(2)}) copy-start(f32[128,4]{0,1:T(4,128)S(1)} %max.140) | copy-start | bytes 6148
  296.8 35.3 %copy-start.84 = (f32[128,4]{0,1:T(4,128)}, f32[128,4]{0,1:T(4,128)S(1)}, u32[]{:S(2)}) copy-start(f32[128,4]{0,1:T(4,128)S(1)} %max.139) | copy-start | bytes 6148
  297.5 34.6 %copy-start.86 = (f32[128,4]{0,1:T(4,128)}, f32[128,4]{0,1:T(4,128)S(1)}, u32[]{:S(2)}) copy-start(f32[128,4]{0,1:T(4,128)S(1)} %max.138) | copy-start | bytes 6148
  298.2 33.9 %copy-start.87 = (f32[128,4]{0,1:T(4,128)}, f32[128,4]{0,1:T(4,128)S(1)}, u32[]{:S(2)}) copy-start(f32[128,4]{0,1:T(4,128)S(1)} %max.137) | copy-start | bytes 6148
  298.9 33.2 %copy-start.88 = (f32[128,4]{0,1:T(4,128)}, f32[128,4]{0,1:T(4,128)S(1)}, u32[]{:S(2)}) copy-start(f32[128,4]{0,1:T(4,128)S(1)} %max.136) | copy-start | bytes 6148
  299.6 32.5 %copy-start.89 = (f32[128,4]{0,1:T(4,128)}, f32[128,4]{0,1:T(4,128)S(1)}, u32[]{:S(2)}) copy-start(f32[128,4]{0,1:T(4,128)S(1)} %max.135) | copy-start | bytes 6148
  315.6 42.1 %copy-start.35 = (f32[128,4,128]{0,2,1:T(8,128)S(1)}, f32[128,4,128]{0,2,1:T(8,128)}, u32[]{:S(2)}) copy-start(f32[128,4,128]{0,2,1:T(8,128)} %copy.281) | copy-start | bytes 786436
  327.0 32.3 %copy-start.33 = (f32[128,4,128]{0,2,1:T(8,128)S(1)}, f32[128,4,128]{0,2,1:T(8,128)}, u32[]{:S(2)}) copy-start(f32[128,4,128]{0,2,1:T(8,128)} %copy.287) | copy-start | bytes 786436
  329.2 82.7 %reduce-scatter.3.cloned.1.call-start = ((), (), s32[]{:S(2)}) async-start(), calls=%async_computation.4 | async-start | bytes 2621440 | tf_op jit(solution)/shard_map/reduce_scatter | solution.py:146
  (81 other events, 923.1 us)
Sparse Core Ops, SparseCore 0:
  9.1 69.0 all-gather.2
  80.0 64.3 all-gather.4
  329.3 32.8 reduce-scatter.4
  367.0 44.8 reduce-scatter.2
where the time goes:
time: 426 us; the launch traced here: 421 us
  waiting for transfers between devices  151 us (35%)
  matrix products  151 us (35%)
  local copies, waits for them, and re-layouts  44.5 us (10%)
  other arithmetic  43.7 us (10%)
  between operations  16.3 us (4%)
  blocking collectives  12.5 us (3%)
    all_gather x1, waiting for transfers between devices, shards(): lax.all_gather(w_value, 'ctx', axis=1, tiled=True)  61.9 us
    reduce_scatter x1, waiting for transfers between devices, shards(): lax.psum_scatter((running_out * factor[..., None]).reshape(query_count, H...  44.2 us
    all_gather x1, waiting for transfers between devices, shards(): lax.all_gather(w_key, 'ctx', axis=1, tiled=True)  43.7 us
    dot_general x32, matrix products, expand_block(): jnp.dot(lat_rows, weight_value, preferred_element_type=jnp.float32)  41.1 us
    dot_general x32, matrix products, expand_block(): jnp.dot(lat_rows, weight_key, preferred_element_type=jnp.float32)  41 us
    dot_general x32, matrix products, expand_block(): jnp.einsum('qhd,kd->qhk', query_rope, rope_keys, preferred_element_type=j...  32.5 us
    while x32, local copies, waits for them, and re-layouts, cached_pass(): return lax.fori_loop(0, block_count, advance, running)  22 us
    dot_general x32, matrix products, expand_block(): jnp.einsum('qhk,khd->qhd', weights.astype(jnp.bfloat16), value_rows, pref...  20.2 us
  transfers between devices with their start and end apart: 4, of which 3 were waited for; matrix products, arithmetic and copies ran while one was open for 16% of the time, Pallas kernels for 0%

commit v1 on v0

--- a/solution.py
+++ b/solution.py
@@ -99,7 +99,9 @@
     live_rows = lengths[0, 0]
     full_key, full_value = (
         lax.all_gather(w_key, "ctx", axis=1, tiled=True),
-        lax.all_gather(w_value, "ctx", axis=1, tiled=True),
+        jnp.concatenate(
+            lax.all_to_all(jnp.stack([w_value] * lax.axis_size("ctx")), "ctx", 0, 0), axis=1
+        ),
     )
     maxima = []
     sums = []

time: 426 us -> 572 us (1.34)
  matrix products: 151 us -> 228 us
  local copies, waits for them, and re-layouts: 44.5 us -> 80.3 us
  other arithmetic: 43.7 us -> 60.4 us
  starting transfers between devices: 0.12 us -> 8.9 us
  waiting for transfers between devices: 151 us -> 159 us
    all_to_all x0 -> x1, waiting for transfers between devices: none -> 101 us  [shards(): lax.all_to_all(jnp.stack([w_value] * lax.axis_size('ctx')), 'ctx', 0, 0)]
    all_gather x1 -> x0, waiting for transfers between devices: 61.9 us -> none  [shards(): lax.all_gather(w_value, 'ctx', axis=1, tiled=True)]
    all_gather x1, waiting for transfers between devices: 43.7 us -> 0.01 us  [shards(): lax.all_gather(w_key, 'ctx', axis=1, tiled=True)]
    dot_general x32, matrix products: 16.5 us -> 37 us  [expand_block(): jnp.einsum('qhd,khd->qhk', query_nope, key_rows, preferred_element_type=j...]
    dot_general x32, matrix products: 32.5 us -> 51.2 us  [expand_block(): jnp.einsum('qhd,kd->qhk', query_rope, rope_keys, preferred_element_type=j...]
    another operation x49 -> x50, local copies, waits for them, and re-layouts: 2.12 us -> 20 us
    dot_general x32, matrix products: 41.1 us -> 56 us  [expand_block(): jnp.dot(lat_rows, weight_value, preferred_element_type=jnp.float32)]
    dot_general x32, matrix products: 41 us -> 52.5 us  [expand_block(): jnp.dot(lat_rows, weight_key, preferred_element_type=jnp.float32)]
  transfers between devices with their start and end apart: 4 -> 4, of which waited for: 3 -> 3; matrix products, arithmetic and copies ran while one was open for 16% -> 22% of each run, Pallas kernels for 0% -> 0%
where the time goes in v1:
time: 572 us; the launch traced here: 564 us
  matrix products  228 us (40%)
  waiting for transfers between devices  159 us (28%)
  local copies, waits for them, and re-layouts  80.3 us (14%)
  other arithmetic  60.4 us (11%)
  between operations  14.6 us (3%)
  blocking collectives  12.5 us (2%)
  starting transfers between devices  8.9 us (2%)
    all_to_all x1, waiting for transfers between devices, shards(): lax.all_to_all(jnp.stack([w_value] * lax.axis_size('ctx')), 'ctx', 0, 0)  101 us
    dot_general x32, matrix products, expand_block(): jnp.dot(lat_rows, weight_value, preferred_element_type=jnp.float32)  56 us
    dot_general x32, matrix products, expand_block(): jnp.dot(lat_rows, weight_key, preferred_element_type=jnp.float32)  52.5 us
    dot_general x32, matrix products, expand_block(): jnp.einsum('qhd,kd->qhk', query_rope, rope_keys, preferred_element_type=j...  51.2 us
    reduce_scatter x1, waiting for transfers between devices, shards(): lax.psum_scatter((running_out * factor[..., None]).reshape(query_count, H...  45.1 us
    dot_general x32, matrix products, expand_block(): jnp.einsum('qhd,khd->qhk', query_nope, key_rows, preferred_element_type=j...  37 us
    dot_general x32, matrix products, expand_block(): jnp.einsum('qhk,khd->qhd', weights.astype(jnp.bfloat16), value_rows, pref...  31.2 us
    while x32, local copies, waits for them, and re-layouts, cached_pass(): return lax.fori_loop(0, block_count, advance, running)  30.4 us
  transfers between devices with their start and end apart: 4, of which 3 were waited for; matrix products, arithmetic and copies ran while one was open for 22% of the time, Pallas kernels for 0%

profile of v1, /device:TPU:1, one launch (start us, length us, event | category | flops | bytes accessed | tf_op | source)
XLA Modules:
  0.0 563.8 jit_solution(12869595617031397651)
XLA Ops:
  10.1 3.9 stack.2
  14.0 8.8 %all-to-all-start = ((bf16[4,512,2048]{1,2,0:T(8,128)(2,1)}), bf16[4,512,2048]{1,2,0:T(8,128)(2,1)}, u32[]{:S(2)}, u32[]{:S(2)}) async-start(bf16[4,512,2048]{1,2,0:T(8,128)(2,1)} %stack.2), calls=%async_computation | async-start | bytes 16777216 | tf_op jit(solution)/shard_map/all_to_all | solution.py:103
  23.6 3.4 copy.204
  60.0 101.5 %all-to-all-done = bf16[4,512,2048]{1,2,0:T(8,128)(2,1)} async-done(((bf16[4,512,2048]{1,2,0:T(8,128)(2,1)}), bf16[4,512,2048]{1,2,0:T(8,128)(2,1)}, u32[]{:S(2)}, u32[]{:S(2)}) %all-to-all-start) | async-done | bytes 8388640 | tf_op jit(solution)/shard_map/all_to_all | solution.py:103
  219.9 3.6 while.256
  229.1 4.9 while.257
  243.9 6.1 %while.258 = (s32[]{:T(128)}, f32[128,4]{0,1:T(4,128)}, f32[128,4]{0,1:T(4,128)}, f32[128,4,128]{2,0,1:T(8,128)S(1)}, s32[]{:T(128)}, /*index=5*/s32[]{:T(128)},...) while((s32[]{:T(128)}, f32[128,4]{0,1:T(4,128)}, ...), condition=%wide.region_13.14_spmd, body=%wide.region_10.13_spmd.sunk | while | flops 85329408 | bytes 3933329 | solution.py:73
  257.1 4.8 while.259
  269.7 6.1 %while.260 = (s32[]{:T(128)}, f32[128,4]{0,1:T(4,128)}, f32[128,4]{0,1:T(4,128)}, f32[128,4,128]{2,0,1:T(8,128)S(1)}, s32[]{:T(128)}, /*index=5*/s32[]{:T(128)},...) while((s32[]{:T(128)}, f32[128,4]{0,1:T(4,128)}, ...), condition=%wide.region_23.24_spmd, body=%wide.region_20.23_spmd.sunk | while | flops 85329408 | bytes 3933329 | solution.py:73
  282.8 4.7 while.261
  295.2 5.9 %while.262 = (s32[]{:T(128)}, f32[128,4]{0,1:T(4,128)}, f32[128,4]{0,1:T(4,128)}, f32[128,4,128]{2,0,1:T(8,128)S(1)}, s32[]{:T(128)}, /*index=5*/s32[]{:T(128)},...) while((s32[]{:T(128)}, f32[128,4]{0,1:T(4,128)}, ...), condition=%wide.region_33.34_spmd, body=%wide.region_30.33_spmd.sunk | while | flops 85329408 | bytes 3933329 | solution.py:73
  308.2 4.8 while.263
  320.2 4.9 while.271
  332.8 6.1 %while.267 = (s32[]{:T(128)}, f32[128,4]{0,1:T(4,128)}, f32[128,4]{0,1:T(4,128)}, f32[128,4,128]{2,0,1:T(8,128)S(1)}, s32[]{:T(128)}, /*index=5*/s32[]{:T(128)},...) while((s32[]{:T(128)}, f32[128,4]{0,1:T(4,128)}, ...), condition=%wide.region_58.59_spmd, body=%wide.region_55.58_spmd.sunk | while | flops 85329408 | bytes 3933329 | solution.py:73
  346.6 6.0 %while.268 = (s32[]{:T(128)}, f32[128,4]{0,1:T(4,128)}, f32[128,4]{0,1:T(4,128)}, f32[128,4,128]{2,0,1:T(8,128)S(1)}, s32[]{:T(128)}, /*index=5*/s32[]{:T(128)},...) while((s32[]{:T(128)}, f32[128,4]{0,1:T(4,128)}, ...), condition=%wide.region_63.64_spmd, body=%wide.region_60.63_spmd.sunk | while | flops 85329408 | bytes 3933329 | solution.py:73
  360.2 7.0 %while.269 = (s32[]{:T(128)}, f32[128,4]{0,1:T(4,128)}, f32[128,4]{0,1:T(4,128)}, f32[128,4,128]{2,0,1:T(8,128)S(1)}, s32[]{:T(128)}, /*index=5*/s32[]{:T(128)},...) while((s32[]{:T(128)}, f32[128,4]{0,1:T(4,128)}, ...), condition=%wide.region_68.69_spmd, body=%wide.region_65.68_spmd.sunk | while | flops 85329408 | bytes 3933329 | solution.py:73
  375.7 7.8 %while.266 = (s32[]{:T(128)}, f32[128,4]{0,1:T(4,128)}, f32[128,4]{0,1:T(4,128)}, f32[128,4,128]{2,0,1:T(8,128)}, s32[]{:T(128)}, /*index=5*/s32[]{:T(128)}, bf1...) while((s32[]{:T(128)}, f32[128,4]{0,1:T(4,128)}, ...), condition=%wide.region_53.54_spmd, body=%wide.region_50.53_spmd.sunk | while | flops 85329408 | bytes 3933329 | solution.py:73
  391.2 7.0 %while.265 = (s32[]{:T(128)}, f32[128,4]{0,1:T(4,128)}, f32[128,4]{0,1:T(4,128)}, f32[128,4,128]{2,0,1:T(8,128)S(1)}, s32[]{:T(128)}, /*index=5*/s32[]{:T(128)},...) while((s32[]{:T(128)}, f32[128,4]{0,1:T(4,128)}, ...), condition=%wide.region_48.49_spmd, body=%wide.region_45.48_spmd.sunk | while | flops 85329408 | bytes 3933329 | solution.py:73
  406.7 7.7 %while.264 = (s32[]{:T(128)}, f32[128,4]{0,1:T(4,128)}, f32[128,4]{0,1:T(4,128)}, f32[128,4,128]{2,0,1:T(8,128)}, s32[]{:T(128)}, /*index=5*/s32[]{:T(128)}, bf1...) while((s32[]{:T(128)}, f32[128,4]{0,1:T(4,128)}, ...), condition=%wide.region_43.44_spmd, body=%wide.region_40.43_spmd.sunk | while | flops 85329408 | bytes 3933329 | solution.py:73
  422.1 6.2 %while.270 = (s32[]{:T(128)}, f32[128,4]{0,1:T(4,128)}, f32[128,4]{0,1:T(4,128)}, f32[128,4,128]{2,0,1:T(8,128)S(1)}, s32[]{:T(128)}, /*index=5*/s32[]{:T(128)},...) while((s32[]{:T(128)}, f32[128,4]{0,1:T(4,128)}, ...), condition=%wide.region_73.74_spmd, body=%wide.region_70.73_spmd.sunk | while | flops 85329408 | bytes 3933329 | solution.py:73
  454.0 12.5 %pmax.7 = bf16[128,64]{0,1:T(8,128)(2,1)S(1)} all-reduce(bf16[128,64]{0,1:T(8,128)(2,1)S(1)} %convert_element_type.488), channel_id=1, replica_groups=mesh['req'=64,'ctx'=4] {'ctx'}, use_global_device_ids=true, to_apply=%region_80.81 | all-reduce | flops 8192 | bytes 32768 | tf_op jit(solution)/shard_map/pmax | solution.py:145
  494.5 3.0 copy.302
  497.5 11.4 %reduce-scatter.5.cloned.1.call-done = bf16[128,16]{0,1:T(8,128)(2,1)} async-done(((bf16[128,64]{0,1:T(8,128)(2,1)}), bf16[128,16]{0,1:T(8,128)(2,1)}) %reduce-scatter.5.cloned.1.call-update) | async-done | bytes 4112 | tf_op jit(solution)/shard_map/reduce_scatter | solution.py:154
  509.7 45.1 %reduce-scatter.3.cloned.1.call-done = bf16[128,2048]{1,0:T(8,128)(2,1)} async-done(((bf16[128,8192]{1,0:T(8,128)(2,1)}), bf16[128,2048]{1,0:T(8,128)(2,1)}) %reduce-scatter.3.cloned.1.call-update) | async-done | bytes 524304 | tf_op jit(solution)/shard_map/reduce_scatter | solution.py:148
  (432 shorter events, 359.2 us)
Async XLA Ops:
  6.5 185.6 %copy-start = (bf16[1,256,512]{2,1,0:T(8,128)(2,1)S(1)}, bf16[1,256,512]{2,1,0:T(8,128)(2,1)}, u32[]{:S(2)}) copy-start(bf16[1,256,512]{2,1,0:T(8,128)(2,1)} %param.43) | copy-start | bytes 786436
  6.5 211.2 %all-gather.2.cloned.1.call-start = ((), (), s32[]{:S(2)}) async-start(), calls=%async_computation.3 | async-start | bytes 10485760 | tf_op jit(solution)/shard_map/all_gather | solution.py:101
  14.0 147.5 %all-to-all-start = ((bf16[4,512,2048]{1,2,0:T(8,128)(2,1)}), bf16[4,512,2048]{1,2,0:T(8,128)(2,1)}, u32[]{:S(2)}, u32[]{:S(2)}) async-start(bf16[4,512,2048]{1,2,0:T(8,128)(2,1)} %stack.2), calls=%async_computation | async-start | bytes 16777216 | tf_op jit(solution)/shard_map/all_to_all | solution.py:103
  22.9 486.0 %reduce-scatter.5.cloned.1.call-start = ((), (), s32[]{:S(2)}) async-start(), calls=%async_computation.5 | async-start | bytes 20480 | tf_op jit(solution)/shard_map/reduce_scatter | solution.py:154
  23.5 138.0 %copy-start.2 = (bf16[1,32,512]{2,1,0:T(8,128)(2,1)S(1)}, bf16[1,32,512]{2,1,0:T(8,128)(2,1)}, u32[]{:S(2)}) copy-start(bf16[1,32,512]{2,1,0:T(8,128)(2,1)} %param.45) | copy-start | bytes 98308
  28.0 162.2 %copy-start.6 = (bf16[128,512]{0,1:T(8,128)(2,1)}, bf16[128,512]{0,1:T(8,128)(2,1)S(1)}, u32[]{:S(2)}) copy-start(bf16[128,512]{0,1:T(8,128)(2,1)S(1)} %get-tuple-element.3001) | copy-start | bytes 393220
  28.0 162.2 %copy-start.7 = (bf16[128,512]{0,1:T(8,128)(2,1)}, bf16[128,512]{0,1:T(8,128)(2,1)S(1)}, u32[]{:S(2)}) copy-start(bf16[128,512]{0,1:T(8,128)(2,1)S(1)} %get-tuple-element.3006) | copy-start | bytes 393220
  28.0 162.2 %copy-start.8 = (bf16[128,512]{0,1:T(8,128)(2,1)}, bf16[128,512]{0,1:T(8,128)(2,1)S(1)}, u32[]{:S(2)}) copy-start(bf16[128,512]{0,1:T(8,128)(2,1)S(1)} %get-tuple-element.3005) | copy-start | bytes 393220
  28.0 162.2 %copy-start.9 = (bf16[128,512]{0,1:T(8,128)(2,1)}, bf16[128,512]{0,1:T(8,128)(2,1)S(1)}, u32[]{:S(2)}) copy-start(bf16[128,512]{0,1:T(8,128)(2,1)S(1)} %get-tuple-element.3004) | copy-start | bytes 393220
  28.0 162.2 %copy-start.10 = (bf16[128,512]{0,1:T(8,128)(2,1)}, bf16[128,512]{0,1:T(8,128)(2,1)S(1)}, u32[]{:S(2)}) copy-start(bf16[128,512]{0,1:T(8,128)(2,1)S(1)} %get-tuple-element.2999) | copy-start | bytes 393220
  28.0 162.2 %copy-start.11 = (bf16[128,512]{0,1:T(8,128)(2,1)}, bf16[128,512]{0,1:T(8,128)(2,1)S(1)}, u32[]{:S(2)}) copy-start(bf16[128,512]{0,1:T(8,128)(2,1)S(1)} %get-tuple-element.3002) | copy-start | bytes 393220
  28.0 162.2 %copy-start.12 = (bf16[128,512]{0,1:T(8,128)(2,1)}, bf16[128,512]{0,1:T(8,128)(2,1)S(1)}, u32[]{:S(2)}) copy-start(bf16[128,512]{0,1:T(8,128)(2,1)S(1)} %get-tuple-element.3003) | copy-start | bytes 393220
  28.0 162.2 %copy-start.13 = (bf16[128,512]{0,1:T(8,128)(2,1)}, bf16[128,512]{0,1:T(8,128)(2,1)S(1)}, u32[]{:S(2)}) copy-start(bf16[128,512]{0,1:T(8,128)(2,1)S(1)} %get-tuple-element.3000) | copy-start | bytes 393220
  194.9 24.9 %copy-start.1 = (bf16[1,256,64]{1,2,0:T(8,128)(2,1)S(1)}, bf16[1,256,64]{1,2,0:T(8,128)(2,1)}, u32[]{:S(2)}) copy-start(bf16[1,256,64]{1,2,0:T(8,128)(2,1)} %param.44) | copy-start | bytes 98308
  234.0 9.9 %copy-start.19 = (f32[128,4]{0,1:T(4,128)}, f32[128,4]{0,1:T(4,128)S(1)}, u32[]{:S(2)}) copy-start(f32[128,4]{0,1:T(4,128)S(1)} %get-tuple-element.2312) | copy-start | bytes 6148
  261.9 7.7 %copy-start.20 = (f32[128,4]{0,1:T(4,128)}, f32[128,4]{0,1:T(4,128)S(1)}, u32[]{:S(2)}) copy-start(f32[128,4]{0,1:T(4,128)S(1)} %get-tuple-element.2316) | copy-start | bytes 6148
  367.2 8.5 %copy-start.3 = (f32[128,4,128]{2,0,1:T(8,128)}, f32[128,4,128]{2,0,1:T(8,128)S(1)}, u32[]{:S(2)}) copy-start(f32[128,4,128]{2,0,1:T(8,128)S(1)} %get-tuple-element.2335) | copy-start | bytes 786436
  398.2 8.5 %copy-start.4 = (f32[128,4,128]{2,0,1:T(8,128)}, f32[128,4,128]{2,0,1:T(8,128)S(1)}, u32[]{:S(2)}) copy-start(f32[128,4,128]{2,0,1:T(8,128)S(1)} %get-tuple-element.2327) | copy-start | bytes 786436
  432.0 21.2 %copy-start.17 = (f32[128,4]{0,1:T(4,128)S(1)}, f32[128,4]{0,1:T(4,128)}, u32[]{:S(2)}) copy-start(f32[128,4]{0,1:T(4,128)} %get-tuple-element.2338) | copy-start | bytes 6148
  432.0 35.7 %copy-start.15 = (f32[128,4,32]{0,2,1:T(8,128)S(1)}, f32[128,4,32]{0,2,1:T(8,128)}, u32[]{:S(2)}) copy-start(f32[128,4,32]{0,2,1:T(8,128)} %get-tuple-element.3036) | copy-start | bytes 196612
  432.0 41.8 %copy-start.23 = (f32[128,4]{0,1:T(4,128)S(1)}, f32[128,4]{0,1:T(4,128)}, u32[]{:S(2)}) copy-start(f32[128,4]{0,1:T(4,128)} %get-tuple-element.2355) | copy-start | bytes 6148
  438.0 42.3 %copy-start.16 = (f32[128,4,32]{0,2,1:T(8,128)S(1)}, f32[128,4,32]{0,2,1:T(8,128)}, u32[]{:S(2)}) copy-start(f32[128,4,32]{0,2,1:T(8,128)} %get-tuple-element.3042) | copy-start | bytes 196612
  438.0 44.8 %copy-start.14 = (f32[128,4,128]{0,2,1:T(8,128)S(1)}, f32[128,4,128]{0,2,1:T(8,128)}, u32[]{:S(2)}) copy-start(f32[128,4,128]{0,2,1:T(8,128)} %copy.246) | copy-start | bytes 786436
  475.3 79.5 %reduce-scatter.3.cloned.1.call-start = ((), (), s32[]{:S(2)}) async-start(), calls=%async_computation.4 | async-start | bytes 2621440 | tf_op jit(solution)/shard_map/reduce_scatter | solution.py:148
  (5 other events, 32.5 us)
Sparse Core Ops, SparseCore 0:
  9.1 114.0 all-gather.1
  475.4 33.4 reduce-scatter.4
  511.7 43.0 reduce-scatter.2
